TPU v7x, 512 devices: a whole 4x4x16 slice. The times are simulated.
512 devices in a mesh: dp: 32 (over y, z_lo), expert: 16 (over z_hi, x, core).
Axes of the slice: x: 4, y: 4, z: 16 (z_hi: 2, z_lo: 8; z = z_hi * 8 + z_lo), core: 2. Of those that a mesh axis runs over, the one named last changes fastest.
Arguments:
- tokens: bfloat16 [65536, 2048], P(('dp', 'expert')), may hold values from -6 to 6
- choice_rows: int32 [32, 16, 512], P('dp', 'expert'), may hold values from 0 to 2047, as said below
- gate_weights: float32 [32, 16, 512], P('dp', 'expert'), may hold values from 0.1 to 1
- w_gate: bfloat16 [16, 2048, 1024], P('expert', 'dp'), may hold values from -0.125 to 0.125
- w_up: bfloat16 [16, 2048, 1024], P('expert', 'dp'), may hold values from -0.125 to 0.125
- w_down: bfloat16 [16, 1024, 2048], P('expert', 'dp'), may hold values from -0.1875 to 0.1875
Outputs:
- mixed: bfloat16 [65536, 2048], P(('dp', 'expert'))
Inputs may be any that keep to these rules, and one draw needn't show every extreme that they name: `choice_rows`: for each group and expert the 512 numbers are distinct; at most 64 of them lie among the 128 tokens of one device of the group (numbers k * 128 to (k + 1) * 128 - 1 belong to device k of the expert axis), and for every expert and group some device gives exactly 64.
All inputs are finite; a program needn't handle non-finite values.
Results may differ from a plain program's by a relative error of at most 0.0057.
Values may be sent and summed in bfloat16 or wider, within the bound.
A program may use at most 64 MiB of HBM per device.

v0:
```python
import jax
import jax.numpy as jnp
from jax import lax
from jax.sharding import PartitionSpec as P


def per_device(tokens, choice_rows, gate_weights, w_gate, w_up, w_down):
    experts = lax.axis_size("expert")
    tok_dev, width = tokens.shape
    most = tok_dev // 2
    own_rows = choice_rows[0, 0]
    every_rows = lax.all_gather(choice_rows, "expert", axis=1, tiled=True)[0]
    myself = lax.axis_index("expert")
    source = every_rows // tok_dev
    local_rows = every_rows % tok_dev
    hits = (source == myself).astype(jnp.int32)
    ranks = jnp.cumsum(hits, axis=1) - 1
    slot_hot = (
        (ranks[:, :, None] == jnp.arange(most)[None, None, :]) & (hits[:, :, None] > 0)
    ).astype(jnp.bfloat16)
    token_hot = (local_rows[:, :, None] == jnp.arange(tok_dev)[None, None, :]).astype(jnp.bfloat16)
    select = jnp.einsum(
        "ecm,ect->emt", slot_hot, token_hot, preferred_element_type=jnp.float32
    ).astype(jnp.bfloat16)
    own_source = own_rows // tok_dev
    source_hot = (own_source[:, None] == jnp.arange(experts)[None, :]).astype(jnp.int32)
    running = jnp.cumsum(source_hot, axis=0) - 1
    own_rank = jnp.sum(running * source_hot, axis=1)
    position = own_source * most + own_rank
    group_rows = lax.all_gather(tokens, "expert", axis=0, tiled=True)
    picked = jnp.take(group_rows, own_rows, axis=0)
    gate_shard = w_gate[0]
    up_shard = w_up[0]
    columns = picked
    gate_sum = jnp.dot(
        columns,
        lax.all_gather(gate_shard, "dp", axis=0, tiled=True),
        preferred_element_type=jnp.float32,
    )
    up_sum = jnp.dot(
        columns,
        lax.all_gather(up_shard, "dp", axis=0, tiled=True),
        preferred_element_type=jnp.float32,
    )
    hidden = (jax.nn.silu(gate_sum) * up_sum).astype(jnp.bfloat16)
    columns = hidden
    expert_out = jnp.dot(
        columns,
        lax.all_gather(w_down[0], "dp", axis=0, tiled=True),
        preferred_element_type=jnp.float32,
    )
    contribution = (gate_weights[0, 0][:, None] * expert_out).astype(jnp.bfloat16)
    outgoing = jnp.zeros((experts * most, width), jnp.bfloat16).at[position].set(contribution)
    returned = lax.all_to_all(outgoing, "expert", split_axis=0, concat_axis=0, tiled=True)
    mixed = jnp.einsum(
        "emt,emd->td",
        select,
        returned.reshape(experts, most, width),
        preferred_element_type=jnp.float32,
    )
    return mixed.astype(jnp.bfloat16)


def solution(mesh):
    return jax.shard_map(
        per_device,
        mesh=mesh,
        in_specs=(
            P(("dp", "expert"), None),
            P("dp", "expert", None),
            P("dp", "expert", None),
            P("expert", "dp", None),
            P("expert", "dp", None),
            P("expert", "dp", None),
        ),
        out_specs=P(("dp", "expert"), None),
        check_vma=False,
    )
```

profile of v0, /device:TPU:65, one launch (start us, length us, event | category | flops | bytes accessed | tf_op | source)
XLA Modules:
  0.0 1159.9 jit_solution(13358310796173171182)
XLA Ops:
  6.5 0.7 all-gather.8.cloned.1.call-update
  7.3 0.7 all-gather.10.cloned.1.call-update
  8.1 0.7 all-gather.12.cloned.1.call-update
  8.8 0.5 all-gather.14.cloned.1.call-update
  9.3 0.7 add_select_fusion.4
  10.0 1.2 reduce-window.16
  11.2 0.2 slice_reduce_fusion
  11.4 0.7 add_select_fusion.5
  12.1 0.1 fusion.32
  12.2 0.7 compare_select_fusion.1
  12.9 0.7 compare_and_fusion
  13.6 174.8 %all-gather.8.cloned.1.call-done = bf16[2048,2048]{1,0:T(8,128)(2,1)} async-done(((bf16[128,2048]{1,0:T(8,128)(2,1)}), bf16[2048,2048]{1,0:T(8,128)(2,1)}) %all-gather.8.cloned.1.call-update) | async-done | bytes 8388624 | tf_op jit(solution)/shard_map/all_gather | solution.py:30
  188.4 8.9 gather_fusion
  197.3 197.4 %all-gather.10.cloned.1.call-done = bf16[1,2048,1024]{2,1,0:T(8,128)(2,1)} async-done(((bf16[1,64,1024]{2,1,0:T(8,128)(2,1)}), bf16[1,2048,1024]{2,1,0:T(8,128)(2,1)}) %all-gather.10.cloned.1.call-update) | async-done | bytes 4194320 | tf_op jit(solution)/shard_map/all_gather | solution.py:37
  394.7 5.9 fusion.4
  400.7 231.3 %all-gather.12.cloned.1.call-done = bf16[1,2048,1024]{2,1,0:T(8,128)(2,1)} async-done(((bf16[1,64,1024]{2,1,0:T(8,128)(2,1)}), bf16[1,2048,1024]{2,1,0:T(8,128)(2,1)}) %all-gather.12.cloned.1.call-update) | async-done | bytes 4194320 | tf_op jit(solution)/shard_map/all_gather | solution.py:42
  632.0 237.1 %all-gather.14.cloned.1.call-done = bf16[1,1024,2048]{2,1,0:T(8,128)(2,1)} async-done(((bf16[1,32,2048]{2,1,0:T(8,128)(2,1)}), bf16[1,1024,2048]{2,1,0:T(8,128)(2,1)}) %all-gather.14.cloned.1.call-update) | async-done | bytes 4194320 | tf_op jit(solution)/shard_map/all_gather | solution.py:49
  869.1 10.0 multiply_convert_fusion
  879.1 7.4 scatter_custom_fusion
  886.5 34.3 %all-to-all-start = ((bf16[16,64,2048]{2,1,0:T(8,128)(2,1)}), bf16[16,64,2048]{2,1,0:T(8,128)(2,1)}, u32[]{:S(2)}, u32[]{:S(2)}) async-start(bf16[16,64,2048]{2,1,0:T(8,128)(2,1)} %bitcast.88), calls=%async_computation | async-start | bytes 8388608 | tf_op jit(solution)/shard_map/all_to_all | solution.py:54
  920.8 226.1 %all_gather.15 = s32[1,16,512]{2,0,1:T(1,128)S(1)} all-gather(s32[1,1,512]{2,0,1:T(1,128)S(1)} %bitcast.93), channel_id=1, replica_groups=mesh['dp'=32,'expert'=16] {'expert'}, dimensions={1}, use_global_device_ids=true | all-gather | bytes 34816 | tf_op jit(solution)/shard_map/all_gather | solution.py:12
  1146.9 1.2 reduce-window.14
  1148.0 0.2 slice_reduce_fusion.1
  1148.4 5.0 fusion.9
  (19 shorter events, 0.4 us)
Async XLA Ops:
  6.5 181.9 %all-gather.8.cloned.1.call-start = ((), (), s32[]{:S(2)}) async-start(), calls=%async_computation.1 | async-start | bytes 8912896 | tf_op jit(solution)/shard_map/all_gather | solution.py:30
  7.3 387.5 %all-gather.10.cloned.1.call-start = ((), (), s32[]{:S(2)}) async-start(), calls=%async_computation.2 | async-start | bytes 4325376 | tf_op jit(solution)/shard_map/all_gather | solution.py:37
  8.0 624.0 %all-gather.12.cloned.1.call-start = ((), (), s32[]{:S(2)}) async-start(), calls=%async_computation.3 | async-start | bytes 4325376 | tf_op jit(solution)/shard_map/all_gather | solution.py:42
  8.7 860.3 %all-gather.14.cloned.1.call-start = ((), (), s32[]{:S(2)}) async-start(), calls=%async_computation.4 | async-start | bytes 4325376 | tf_op jit(solution)/shard_map/all_gather | solution.py:49
  197.3 671.8 %copy-start.1 = (f32[1,1,512]{2,1,0:T(1,128)S(1)}, f32[1,1,512]{2,1,0:T(1,128)}, u32[]{:S(2)}) copy-start(f32[1,1,512]{2,1,0:T(1,128)} %param.8) | copy-start | bytes 6148
  886.5 34.3 %copy-start = (s32[1,1,512]{2,1,0:T(1,128)S(1)}, s32[1,1,512]{2,1,0:T(1,128)}, u32[]{:S(2)}) copy-start(s32[1,1,512]{2,1,0:T(1,128)} %param.7) | copy-start | bytes 6148
  886.5 262.0 %all-to-all-start = ((bf16[16,64,2048]{2,1,0:T(8,128)(2,1)}), bf16[16,64,2048]{2,1,0:T(8,128)(2,1)}, u32[]{:S(2)}, u32[]{:S(2)}) async-start(bf16[16,64,2048]{2,1,0:T(8,128)(2,1)} %bitcast.88), calls=%async_computation | async-start | bytes 8388608 | tf_op jit(solution)/shard_map/all_to_all | solution.py:54
Sparse Core Ops, SparseCore 0:
  10.6 177.7 all-gather.7
  190.5 204.1 all-gather.9
  396.8 235.1 all-gather.11
  633.9 235.1 all-gather.13
where the time goes:
time: 1160 us
  waiting for transfers between devices  843 us (73%)
  blocking collectives  226 us (19%)
  starting transfers between devices  34.4 us (3%)
  matrix products  20.9 us (2%)
  local copies, waits for them, and re-layouts  16.7 us (1%)
  between operations  13.2 us (1%)
    all_gather x1, waiting for transfers between devices, per_device(): lax.all_gather(w_down[0], 'dp', axis=0, tiled=True)  237 us
    all_gather x1, waiting for transfers between devices, per_device(): lax.all_gather(up_shard, 'dp', axis=0, tiled=True)  231 us
    all_gather x1, blocking collectives, per_device(): every_rows = lax.all_gather(choice_rows, 'expert', axis=1, tiled=True)[0]  226 us
    all_gather x1, waiting for transfers between devices, per_device(): lax.all_gather(gate_shard, 'dp', axis=0, tiled=True)  197 us
    all_gather x1, waiting for transfers between devices, per_device(): group_rows = lax.all_gather(tokens, 'expert', axis=0, tiled=True)  175 us
    all_to_all x1, starting transfers between devices, per_device(): lax.all_to_all(outgoing, 'expert', split_axis=0, concat_axis=0, tiled=True)  34.3 us
  transfers between devices with their start and end apart: 5, of which 4 were waited for; matrix products, arithmetic and copies ran while one was open for 2% of the time, Pallas kernels for 0%

commit v1 on v0

v1 whole, which is shorter than its diff:
```python
import functools

import jax
import jax.numpy as jnp
from jax import lax
from jax.experimental import pallas as pl
from jax.experimental.pallas import tpu as pltpu
from jax.sharding import PartitionSpec as P

MESH = pl.DeviceIdType.MESH
Y = 4
X = 4
NC = 4
BF = jnp.bfloat16
F32 = jnp.float32


def remote(src, dst, send_sem, recv_sem, device):
    return pltpu.make_async_remote_copy(
        src_ref=src,
        dst_ref=dst,
        send_sem=send_sem,
        recv_sem=recv_sem,
        device_id=device,
        device_id_type=MESH,
    )


def layer_kernel(
    ZL,
    tin, gu_in, dn_in, rows_col, rows_row, gw_col,
    out,
    tok, gu, dn, oh, oht, picked, hidden, contrib, dense,
    rz, prcv, xrl, xf, zsend, zrel, zfin,
    gsem, dsem, tsem, xsem, psem, csem,
):
    T, D = tin.shape
    H = gu.shape[1] // 2
    CAP = rows_col.shape[0]
    CW = D // NC
    T2 = T // 2
    dp = lax.axis_index("dp")
    ex = lax.axis_index("expert")
    y, k = dp // ZL, dp % ZL
    zh, x, c = ex // (2 * X), (ex // 2) % X, ex % 2
    z = zh * ZL + k
    oz = 1 - zh
    yp, ym, y2 = (y + 1) % Y, (y + 3) % Y, (y + 2) % Y
    xp, xm, x2 = (x + 1) % X, (x + 3) % X, (x + 2) % X
    zq = ((z + ZL // 2) % (2 * ZL), (z + 2 * ZL - ZL // 2) % (2 * ZL))

    def dev(y_=y, k_=k, zh_=zh, x_=x, c_=c):
        return (y_ * ZL + k_, zh_ * (2 * X) + x_ * 2 + c_)

    dev_y = (dev(y_=yp), dev(y_=ym))
    dev_x = (dev(x_=xp), dev(x_=xm))
    dev_z = (dev(k_=k + 1), dev(k_=k - 1))
    dev_q = tuple(dev(k_=v % ZL, zh_=v // ZL) for v in zq)
    dev_c = dev(c_=1 - c)
    has_z = (k < ZL - 1, k > 0)

    barrier = pltpu.get_barrier_semaphore()
    for peer in dev_y + dev_x + dev_q + (dev_c,):
        pl.semaphore_signal(barrier, inc=1, device_id=peer, device_id_type=MESH)
    for d in range(2):
        @pl.when(has_z[d])
        def _():
            pl.semaphore_signal(barrier, inc=1, device_id=dev_z[d], device_id_type=MESH)
    pl.semaphore_wait(barrier, 7 + jnp.where(k < ZL - 1, 1, 0) + jnp.where(k > 0, 1, 0))

    class Part:
        def __init__(self, own, buf, sem):
            self.own, self.buf, self.sem = own, buf, sem
            self.R = own.shape[0]

        def rows(self, y_, j, half=None):
            R = self.R
            if half is None:
                return self.buf.at[pl.ds(pl.multiple_of((y_ * ZL + j) * R, R), R)]
            h = R // 2
            return self.buf.at[pl.ds(pl.multiple_of((y_ * ZL + j) * R + half * h, h), h)]

        def z_send(self, src, j, d):
            remote(src, self.rows(y, j), self.sem.at[1 + d, j], self.sem.at[0, j], dev_z[d]).start()

        def y_send(self, src, j):
            for d in range(2):
                remote(src, self.rows(y, j), self.sem.at[3 + d, j], self.sem.at[5 + d, j], dev_y[d]).start()

        def wait(self, ref, i, j):
            remote(ref, ref, self.sem.at[1, j], self.sem.at[i, j], dev_c).wait_recv()

        def wait_sent(self, ref, i, j):
            remote(ref, ref, self.sem.at[i, j], self.sem.at[0, j], dev_c).wait_send()

        def z_step(self, s, with_y):
            for d, j in ((0, k - s), (1, k + s)):
                @pl.when((j >= 0) & (j < ZL))
                def _():
                    ref = self.rows(y, j)
                    self.wait(ref, 0, j)
                    @pl.when(has_z[d])
                    def _():
                        self.z_send(ref, j, d)
                    if with_y:
                        self.y_send(ref, j)

        def y_step(self, s):
            for d, j in ((0, k - s), (1, k + s)):
                ok = (j >= 0) & (j < ZL)
                if d == 1:
                    ok = ok & (s > 0)
                @pl.when(ok)
                def _():
                    @pl.when(s > 0)
                    def _():
                        self.y_send(self.rows(y, j), j)
                    @pl.when(s == 0)
                    def _():
                        self.y_send(self.own, j)

        def relay_step(self, s):
            for d, j in ((0, k - s), (1, k + s)):
                ok = (j >= 0) & (j < ZL)
                if d == 1:
                    ok = ok & (s > 0)
                @pl.when(ok)
                def _():
                    for e, y_ in ((0, ym), (1, yp)):
                        self.wait(self.rows(y_, j), 5 + e, j)
                        half = self.rows(y_, j, e)
                        remote(half, half, self.sem.at[7 + e, j], self.sem.at[9 + e, j], dev_y[e]).start()

        def arrived(self):
            @pl.loop(0, ZL)
            def _(j):
                for e in range(2):
                    self.wait(self.rows(y2, j, e), 9 + e, j)

        def drain(self):
            @pl.loop(0, ZL)
            def _(j):
                ref = self.rows(y, j)
                for d in range(2):
                    self.wait_sent(ref, 3 + d, j)
                    self.wait_sent(self.rows(y, j, 0), 7 + d, j)
                    ok = has_z[d] & ((j <= k) if d == 0 else (j >= k))
                    @pl.when(ok)
                    def _():
                        self.wait_sent(ref, 1 + d, j)

    G = Part(gu_in, gu, gsem)
    W = Part(dn_in, dn, dsem)

    def blk(c_, x_, q_):
        b = c_ * (2 * X) + x_ * 2 + q_
        return tok.at[pl.ds(pl.multiple_of(b * T, T), T)]

    def blk_half(c_, x_, q_, h):
        b = c_ * (2 * X) + x_ * 2 + q_
        return tok.at[pl.ds(pl.multiple_of(b * T + h * T2, T2), T2)]

    def wait_on(ref, sem):
        remote(ref, ref, sem, sem, dev_c).wait_recv()

    def wait_sent_on(ref, sem):
        remote(ref, ref, sem, sem, dev_c).wait_send()

    def x_send(src, q):
        for d in range(2):
            remote(src, blk(c, x, q), xsem.at[d, q], xsem.at[2 + d, q], dev_x[d]).start()

    def to_partner(src, r, q):
        x_ = (x + r) % X
        remote(src, blk(c, x_, q), psem.at[0, r * 2 + q], psem.at[1, r * 2 + q], dev_c).start()

    def x_arrivals(q):
        for d, r in ((0, 3), (1, 1)):
            ref = blk(c, (x + r) % X, q)
            wait_on(ref, xsem.at[2 + d, q])
            @pl.when(q == d)
            def _():
                remote(ref, ref, xsem.at[4, q], xsem.at[5, q], dev_x[d]).start()
            to_partner(ref, r, q)

    def x_far(q):
        ref = blk(c, x2, q)
        wait_on(ref, xsem.at[5, q])
        to_partner(ref, 2, q)

    def tok_leg1():
        for d in range(2):
            remote(tin.at[pl.ds(d * T2, T2)], rz.at[d], tsem.at[0, d], tsem.at[1, d], dev_q[d]).start()

    def tok_leg2():
        for d in range(2):
            wait_on(rz.at[d], tsem.at[1, d])
            far = 1 - zq[d] // ZL
            remote(rz.at[d], blk_half(c, x, far, d), tsem.at[2, d], tsem.at[3, d], dev_q[d]).start()

    def tok_opp():
        for d in range(2):
            wait_on(blk_half(c, x, oz, d), tsem.at[3, d])
        x_send(blk(c, x, oz), oz)
        to_partner(blk(c, x, oz), 0, oz)

    for d in range(2):
        @pl.when(has_z[d])
        def _():
            G.z_send(gu_in, k, d)
    G.y_send(gu_in, k)
    tok_leg1()
    x_send(tin, zh)
    to_partner(tin, 0, zh)
    for d in range(2):
        @pl.when(has_z[d])
        def _():
            W.z_send(dn_in, k, d)

    gu[pl.ds(pl.multiple_of(dp * gu_in.shape[0], gu_in.shape[0]), gu_in.shape[0]), :] = gu_in[...]
    dn[pl.ds(pl.multiple_of(dp * dn_in.shape[0], dn_in.shape[0]), dn_in.shape[0]), :] = dn_in[...]
    tok[pl.ds(pl.multiple_of((c * 2 * X + x * 2 + zh) * T, T), T), :] = tin[...]

    G.z_step(1, True)

    NB = 2 * X * 2

    @pl.loop(0, NB)
    def _(b):
        off = pl.multiple_of(b * T, T)
        lanes = lax.broadcasted_iota(jnp.int32, (CAP, T), 1) + b * T
        oh[:, pl.ds(off, T)] = jnp.where(rows_col[...] == lanes, 1.0, 0.0).astype(BF)
        subs = lax.broadcasted_iota(jnp.int32, (T, CAP), 0) + b * T
        oht[pl.ds(off, T), :] = jnp.where(rows_row[...] == subs, 1.0, 0.0).astype(BF)

    G.z_step(2, True)
    W.z_step(1, False)
    x_arrivals(zh)
    tok_leg2()
    G.z_step(3, True)
    W.z_step(2, False)
    G.relay_step(0)
    W.y_step(0)
    x_far(zh)
    G.z_step(4, True)
    W.z_step(3, False)
    G.relay_step(1)
    W.y_step(1)
    tok_opp()
    G.z_step(5, True)
    W.z_step(4, False)
    G.relay_step(2)
    W.y_step(2)
    G.z_step(6, True)
    W.z_step(5, False)
    G.relay_step(3)
    W.y_step(3)
    x_arrivals(oz)
    G.z_step(7, True)
    W.z_step(6, False)
    G.relay_step(4)
    W.y_step(4)
    W.z_step(7, False)
    G.relay_step(5)
    W.y_step(5)
    x_far(oz)

    @pl.loop(6, 8)
    def _(s):
        G.relay_step(s)
        W.y_step(s)

    for r in range(X):
        for q in range(2):
            wait_on(blk(1 - c, (x + r) % X, q), psem.at[1, r * 2 + q])

    TN = min(256, D)

    @pl.loop(0, D // TN)
    def _(n):
        cols = pl.ds(pl.multiple_of(n * TN, TN), TN)
        picked[:, cols] = jnp.dot(oh[...], tok[:, cols], preferred_element_type=F32).astype(BF)

    @pl.loop(0, 4)
    def _(s):
        W.relay_step(s)

    G.arrived()
    TH = min(256, H)

    @pl.loop(0, H // TH)
    def _(n):
        ga = jnp.dot(picked[...], gu[:, pl.ds(pl.multiple_of(n * TH, TH), TH)], preferred_element_type=F32)
        ub = jnp.dot(picked[...], gu[:, pl.ds(pl.multiple_of(H + n * TH, TH), TH)], preferred_element_type=F32)
        hidden[:, pl.ds(pl.multiple_of(n * TH, TH), TH)] = (ga / (1.0 + jnp.exp(-ga)) * ub).astype(BF)

    @pl.loop(4, 8)
    def _(s):
        W.relay_step(s)

    W.arrived()

    HB = 2 * X * T
    TM = min(256, HB)

    def s1(n):
        cols = pl.ds(pl.multiple_of(n * CW, CW), CW)
        o = jnp.dot(hidden[...], dn[:, cols], preferred_element_type=F32)
        contrib[...] = (gw_col[...] * o).astype(BF)

        def spread(base):
            @pl.loop(0, HB // TM)
            def _(m):
                r = pl.ds(pl.multiple_of(base + m * TM, TM), TM)
                dense[n, r, :] = jnp.dot(oht[r, :], contrib[...], preferred_element_type=F32).astype(BF)

        theirs = pl.multiple_of((1 - c) * HB, HB)
        spread(theirs)
        remote(dense.at[n, pl.ds(theirs, HB)], prcv.at[n], csem.at[n, 0], csem.at[n, 1], dev_c).start()
        spread(pl.multiple_of(c * HB, HB))

    def pblk(n, x_, q_, count=1):
        return prcv.at[n, pl.ds(pl.multiple_of((x_ * 2 + q_) * T, T), count * T)]

    def s2(n):
        wait_on(prcv.at[n], csem.at[n, 1])

        @pl.loop(0, 2 * X)
        def _(b):
            r = pl.ds(pl.multiple_of(b * T, T), T)
            mine = dense[n, pl.ds(pl.multiple_of(c * HB + b * T, T), T), :]
            prcv[n, r, :] = (prcv[n, r, :].astype(F32) + mine.astype(F32)).astype(BF)

        for d in range(2):
            remote(pblk(n, x2, d), xrl.at[d, n], csem.at[n, 2 + d], csem.at[n, 4 + d], dev_x[d]).start()

    def s3(n):
        for d, x_ in ((0, xp), (1, xm)):
            wait_on(xrl.at[d, n], csem.at[n, 4 + d])
            r = pl.ds(pl.multiple_of((x_ * 2 + d) * T, T), T)
            prcv[n, r, :] = (prcv[n, r, :].astype(F32) + xrl[d, n].astype(F32)).astype(BF)
            remote(pblk(n, x_, 0, 2), xf.at[d, n], csem.at[n, 6 + d], csem.at[n, 8 + d], dev_x[d]).start()

    def total(n, q):
        r = pl.ds(pl.multiple_of((x * 2 + q) * T, T), T)
        g = pl.ds(pl.multiple_of(q * T, T), T)
        return prcv[n, r, :].astype(F32) + xf[0, n, g, :].astype(F32) + xf[1, n, g, :].astype(F32)

    def s4(n):
        for d in range(2):
            wait_on(xf.at[d, n], csem.at[n, 8 + d])
        zsend[n] = total(n, oz).astype(BF)
        for d in range(2):
            remote(zsend.at[n, pl.ds(d * T2, T2)], zrel.at[d, n], csem.at[n, 10 + d], csem.at[n, 12 + d], dev_q[d]).start()

    def s5(n):
        for d in range(2):
            wait_on(zrel.at[d, n], csem.at[n, 12 + d])
            remote(zrel.at[d, n], zfin.at[n, pl.ds(d * T2, T2)], csem.at[n, 14 + d], csem.at[n, 16 + d], dev_q[d]).start()

    def s6(n):
        for d in range(2):
            wait_on(zfin.at[n, pl.ds(d * T2, T2)], csem.at[n, 16 + d])
        out[:, pl.ds(pl.multiple_of(n * CW, CW), CW)] = (total(n, zh) + zfin[n].astype(F32)).astype(BF)

    stages = (s1, s2, s3, s4, s5, s6)

    @pl.loop(0, NC + len(stages) - 1)
    def _(t):
        for i in reversed(range(len(stages))):
            @pl.when((t >= i) & (t < NC + i))
            def _():
                stages[i](t - i)

    G.drain()
    W.drain()
    for d in range(2):
        wait_sent_on(rz.at[d], tsem.at[0, d])
        wait_sent_on(rz.at[d], tsem.at[2, d])
    for q in range(2):
        for i in (0, 1, 4):
            wait_sent_on(tin, xsem.at[i, q])
        for r in range(X):
            wait_sent_on(tin, psem.at[0, r * 2 + q])

    @pl.loop(0, NC)
    def _(n):
        wait_sent_on(prcv.at[n], csem.at[n, 0])
        for d in range(2):
            wait_sent_on(xrl.at[d, n], csem.at[n, 2 + d])
            wait_sent_on(xf.at[d, n], csem.at[n, 6 + d])
            wait_sent_on(zrel.at[d, n], csem.at[n, 10 + d])
            wait_sent_on(zrel.at[d, n], csem.at[n, 14 + d])


def per_device(ZL, tokens, choice_rows, gate_weights, w_gate, w_up, w_down):
    T, D = tokens.shape
    H = w_gate.shape[2]
    CAP = choice_rows.shape[2]
    group = 4 * X * T
    CW = D // NC
    rows = choice_rows[0, 0]
    dev, r = rows // T, rows % T
    zh, x, c = dev // (2 * X), (dev // 2) % X, dev % 2
    rows = (c * (2 * X) + x * 2 + zh) * T + r
    gu_in = jnp.concatenate([w_gate[0], w_up[0]], axis=1)
    dn_in = w_down[0]
    dps = Y * ZL
    vmem = pl.BlockSpec(memory_space=pltpu.VMEM)
    return pl.pallas_call(
        functools.partial(layer_kernel, ZL),
        out_shape=jax.ShapeDtypeStruct((T, D), BF),
        in_specs=[vmem] * 6,
        out_specs=vmem,
        scratch_shapes=[
            pltpu.VMEM((group, D), BF),
            pltpu.VMEM((dps * gu_in.shape[0], 2 * H), BF),
            pltpu.VMEM((dps * dn_in.shape[0], D), BF),
            pltpu.VMEM((CAP, group), BF),
            pltpu.VMEM((group, CAP), BF),
            pltpu.VMEM((CAP, D), BF),
            pltpu.VMEM((CAP, H), BF),
            pltpu.VMEM((CAP, CW), BF),
            pltpu.VMEM((NC, group, CW), BF),
            pltpu.VMEM((2, T // 2, D), BF),
            pltpu.VMEM((NC, group // 2, CW), BF),
            pltpu.VMEM((2, NC, T, CW), BF),
            pltpu.VMEM((2, NC, 2 * T, CW), BF),
            pltpu.VMEM((NC, T, CW), BF),
            pltpu.VMEM((2, NC, T // 2, CW), BF),
            pltpu.VMEM((NC, T, CW), BF),
            pltpu.SemaphoreType.DMA((11, ZL)),
            pltpu.SemaphoreType.DMA((11, ZL)),
            pltpu.SemaphoreType.DMA((4, 2)),
            pltpu.SemaphoreType.DMA((6, 2)),
            pltpu.SemaphoreType.DMA((2, 8)),
            pltpu.SemaphoreType.DMA((NC, 18)),
        ],
        compiler_params=pltpu.CompilerParams(
            collective_id=0, has_side_effects=True, vmem_limit_bytes=62 * 1024 * 1024
        ),
    )(tokens, gu_in, dn_in, rows.reshape(CAP, 1), rows.reshape(1, CAP), gate_weights.reshape(CAP, 1))


def solution(mesh):
    return jax.shard_map(
        functools.partial(per_device, mesh.shape["dp"] // Y),
        mesh=mesh,
        in_specs=(
            P(("dp", "expert"), None),
            P("dp", "expert", None),
            P("dp", "expert", None),
            P("expert", "dp", None),
            P("expert", "dp", None),
            P("expert", "dp", None),
        ),
        out_specs=P(("dp", "expert"), None),
        check_vma=False,
    )
```

time: 1160 us -> 255 us (0.22)
  the two profiles are of different devices: /device:TPU:65 before, /device:TPU:24 now
where the time goes in v1:
time: 255 us
  Pallas kernels  249 us (98%)
  local copies, waits for them, and re-layouts  3.71 us (1%)
  other arithmetic  2.75 us (1%)
    pallas_call x1, Pallas kernels, per_device(): pl.pallas_call(functools.partial(layer_kernel, ZL), out_shape=jax.ShapeDt...  249 us

profile of v1, /device:TPU:24, one launch (start us, length us, event | category | flops | bytes accessed | tf_op | source)
XLA Modules:
  0.0 255.0 jit_solution(10859335201111567219)
XLA Ops:
  0.0 0.0 copy-start.2
  0.0 0.7 copy-done.2
  0.7 0.0 copy-start.3
  0.7 0.6 fusion.13.rows_row
  1.3 0.0 copy-done.3
  1.4 0.0 copy-start
  1.4 0.0 copy-start.1
  1.4 0.9 copy.11.gw_col
  2.2 0.0 copy-done
  2.3 0.1 copy-done.1
  2.3 0.7 pad_maximum_fusion.gu_in
  3.1 0.1 copy.7
  3.2 1.4 fusion.4.rows_col
  4.6 248.5 %shard_map.64 = bf16[128,2048]{1,0:T(8,128)(2,1)} custom-call(bf16[128,2048]{1,0:T(8,128)(2,1)} %tin.1, bf16[64,2048]{1,0:T(8,128)(2,1)} %pad_maximum_fusion.gu_in, bf16[32,2048]{1,0:T(8,128)(2,1)} %bitcast.18, s32[512,1]{1,0:T(8,128)} %fusion.4.rows_col, s32[1,512]{1,0:T(1,128)} %fusion.13.rows_row, f32[512,1]{1,0:T(8,128)} %copy.11.gw_col), custom_call_target="tpu_custom_call" | custom-call | tf_op jit(solution)/shard_map/pallas_call | solution.py:410
  253.1 1.9 copy.13
Async XLA Ops:
  0.0 0.7 copy-start.2
  0.7 0.7 copy-start.3
  1.4 0.9 copy-start
  1.4 1.0 copy-start.1

commit v2 on v1

--- a/solution.py
+++ b/solution.py
@@ -11,6 +11,7 @@
 Y = 4
 X = 4
 NC = 4
+NP = 4
 BF = jnp.bfloat16
 F32 = jnp.float32
 
@@ -28,15 +29,16 @@
 
 def layer_kernel(
     ZL,
-    tin, gu_in, dn_in, rows_col, rows_row, gw_col,
+    tin, wg_in, wu_in, dn_in, rows_ref, gw_ref,
     out,
-    tok, gu, dn, oh, oht, picked, hidden, contrib, dense,
+    gw_col, tok, gu, dn, oh, oht, picked, hidden, contrib, dense,
     rz, prcv, xrl, xf, zsend, zrel, zfin,
-    gsem, dsem, tsem, xsem, psem, csem,
+    gsem, dsem, lsem, xsem, rsem, psem, xown, pown, csem,
 ):
     T, D = tin.shape
     H = gu.shape[1] // 2
-    CAP = rows_col.shape[0]
+    CAP = rows_ref.shape[1]
+    R = wg_in.shape[0]
     CW = D // NC
     T2 = T // 2
     dp = lax.axis_index("dp")
@@ -58,6 +60,11 @@
     dev_q = tuple(dev(k_=v % ZL, zh_=v // ZL) for v in zq)
     dev_c = dev(c_=1 - c)
     has_z = (k < ZL - 1, k > 0)
+
+    own_rows = pl.ds(pl.multiple_of(dp * R, R), R)
+    gu[own_rows, :H] = wg_in[...]
+    gu[own_rows, H:] = wu_in[...]
+    gu_own = gu.at[own_rows]
 
     barrier = pltpu.get_barrier_semaphore()
     for peer in dev_y + dev_x + dev_q + (dev_c,):
@@ -149,16 +156,18 @@
                     def _():
                         self.wait_sent(ref, 1 + d, j)
 
-    G = Part(gu_in, gu, gsem)
+    G = Part(gu_own, gu, gsem)
     W = Part(dn_in, dn, dsem)
 
     def blk(c_, x_, q_):
-        b = c_ * (2 * X) + x_ * 2 + q_
+        b = q_ * (2 * X) + c_ * X + x_
         return tok.at[pl.ds(pl.multiple_of(b * T, T), T)]
 
-    def blk_half(c_, x_, q_, h):
-        b = c_ * (2 * X) + x_ * 2 + q_
-        return tok.at[pl.ds(pl.multiple_of(b * T + h * T2, T2), T2)]
+    TP = T2 // NP
+
+    def piece(c_, x_, q_, h, p):
+        b = q_ * (2 * X) + c_ * X + x_
+        return tok.at[pl.ds(pl.multiple_of(b * T + h * T2 + p * TP, TP), TP)]
 
     def wait_on(ref, sem):
         remote(ref, ref, sem, sem, dev_c).wait_recv()
@@ -166,124 +175,182 @@
     def wait_sent_on(ref, sem):
         remote(ref, ref, sem, sem, dev_c).wait_send()
 
-    def x_send(src, q):
-        for d in range(2):
-            remote(src, blk(c, x, q), xsem.at[d, q], xsem.at[2 + d, q], dev_x[d]).start()
-
-    def to_partner(src, r, q):
-        x_ = (x + r) % X
-        remote(src, blk(c, x_, q), psem.at[0, r * 2 + q], psem.at[1, r * 2 + q], dev_c).start()
-
-    def x_arrivals(q):
+    def half(ref, d):
+        return ref.at[pl.ds(d * T2, T2)]
+
+    def own_start():
+        for d in range(2):
+            remote(tin, blk(c, x, zh), xown.at[0, d], xown.at[1, d], dev_x[d]).start()
+        remote(tin, blk(c, x, zh), pown.at[0, 0], pown.at[1, 0], dev_c).start()
+
+    def own_arrivals():
         for d, r in ((0, 3), (1, 1)):
-            ref = blk(c, (x + r) % X, q)
-            wait_on(ref, xsem.at[2 + d, q])
-            @pl.when(q == d)
-            def _():
-                remote(ref, ref, xsem.at[4, q], xsem.at[5, q], dev_x[d]).start()
-            to_partner(ref, r, q)
-
-    def x_far(q):
-        ref = blk(c, x2, q)
-        wait_on(ref, xsem.at[5, q])
-        to_partner(ref, 2, q)
-
-    def tok_leg1():
-        for d in range(2):
-            remote(tin.at[pl.ds(d * T2, T2)], rz.at[d], tsem.at[0, d], tsem.at[1, d], dev_q[d]).start()
-
-    def tok_leg2():
-        for d in range(2):
-            wait_on(rz.at[d], tsem.at[1, d])
-            far = 1 - zq[d] // ZL
-            remote(rz.at[d], blk_half(c, x, far, d), tsem.at[2, d], tsem.at[3, d], dev_q[d]).start()
-
-    def tok_opp():
-        for d in range(2):
-            wait_on(blk_half(c, x, oz, d), tsem.at[3, d])
-        x_send(blk(c, x, oz), oz)
-        to_partner(blk(c, x, oz), 0, oz)
+            ref = blk(c, (x + r) % X, zh)
+            wait_on(ref, xown.at[1, d])
+            part = half(ref, d)
+            remote(part, part, xown.at[2, d], xown.at[3, d], dev_x[d]).start()
+            remote(ref, ref, pown.at[0, r], pown.at[1, r], dev_c).start()
+
+    def own_far():
+        ref = blk(c, x2, zh)
+        for d in range(2):
+            wait_on(half(ref, d), xown.at[3, d])
+        remote(ref, ref, pown.at[0, 2], pown.at[1, 2], dev_c).start()
+
+    def leg1(p):
+        for d in range(2):
+            own = tin.at[pl.ds(pl.multiple_of(d * T2 + p * TP, TP), TP)]
+            dst = rz.at[d, pl.ds(pl.multiple_of(p * TP, TP), TP)]
+            remote(own, dst, lsem.at[0, d, p], lsem.at[1, d, p], dev_q[d]).start()
+
+    def leg2(p):
+        for d in range(2):
+            mid = rz.at[d, pl.ds(pl.multiple_of(p * TP, TP), TP)]
+            wait_on(mid, lsem.at[1, d, p])
+            dst = piece(c, x, 1 - zq[d] // ZL, d, p)
+            remote(mid, dst, lsem.at[2, d, p], lsem.at[3, d, p], dev_q[d]).start()
+
+    def to_partner(ref, r, h, p):
+        remote(ref, ref, psem.at[0, r * 2 + h, p], psem.at[1, r * 2 + h, p], dev_c).start()
+
+    def opp_arrived(p):
+        for h in range(2):
+            ref = piece(c, x, oz, h, p)
+            wait_on(ref, lsem.at[3, h, p])
+            for d in range(2):
+                remote(ref, ref, xsem.at[d, h, p], xsem.at[2 + d, h, p], dev_x[d]).start()
+            to_partner(ref, 0, h, p)
+
+    def opp_x(p):
+        for d, r in ((0, 3), (1, 1)):
+            for h in (d, 1 - d):
+                ref = piece(c, (x + r) % X, oz, h, p)
+                wait_on(ref, xsem.at[2 + d, h, p])
+                if h == d:
+                    remote(ref, ref, rsem.at[0, h, p], rsem.at[1, h, p], dev_x[d]).start()
+                to_partner(ref, r, h, p)
+
+    def opp_far(p):
+        for h in range(2):
+            ref = piece(c, x2, oz, h, p)
+            wait_on(ref, rsem.at[1, h, p])
+            to_partner(ref, 2, h, p)
 
     for d in range(2):
         @pl.when(has_z[d])
         def _():
-            G.z_send(gu_in, k, d)
-    G.y_send(gu_in, k)
-    tok_leg1()
-    x_send(tin, zh)
-    to_partner(tin, 0, zh)
-    for d in range(2):
-        @pl.when(has_z[d])
+            G.z_send(gu_own, k, d)
+    G.y_send(gu_own, k)
+    own_start()
+
+    dn[pl.ds(pl.multiple_of(dp * dn_in.shape[0], dn_in.shape[0]), dn_in.shape[0]), :] = dn_in[...]
+    tok[pl.ds(pl.multiple_of((zh * 2 * X + c * X + x) * T, T), T), :] = tin[...]
+
+    NB = 2 * X * 2
+
+    def hots():
+        rows = rows_ref[...]
+        lt = T.bit_length() - 1
+        r = rows & (T - 1)
+        core = (rows >> lt) & 1
+        xx = (rows >> (lt + 1)) & (X - 1)
+        hh = rows >> (lt + 3)
+        rows_in = (hh * (2 * X) + core * X + xx) * T + r
+        rows_out = (core * (2 * X) + xx * 2 + hh) * T + r
+        rows_col = jnp.broadcast_to(rows_in, (8, CAP)).T[:, 0:1]
+        gw_col[...] = jnp.broadcast_to(gw_ref[...], (8, CAP)).T[:, 0:1]
+
+        @pl.loop(0, NB)
+        def _(b):
+            off = pl.multiple_of(b * T, T)
+            lanes = lax.broadcasted_iota(jnp.int32, (CAP, T), 1) + b * T
+            oh[:, pl.ds(off, T)] = jnp.where(rows_col == lanes, 1.0, 0.0).astype(BF)
+            subs = lax.broadcasted_iota(jnp.int32, (T, CAP), 0) + b * T
+            oht[pl.ds(off, T), :] = jnp.where(rows_out == subs, 1.0, 0.0).astype(BF)
+
+    def when_in(s, lo, hi, f):
+        @pl.when((s >= lo) & (s < hi))
         def _():
-            W.z_send(dn_in, k, d)
-
-    gu[pl.ds(pl.multiple_of(dp * gu_in.shape[0], gu_in.shape[0]), gu_in.shape[0]), :] = gu_in[...]
-    dn[pl.ds(pl.multiple_of(dp * dn_in.shape[0], dn_in.shape[0]), dn_in.shape[0]), :] = dn_in[...]
-    tok[pl.ds(pl.multiple_of((c * 2 * X + x * 2 + zh) * T, T), T), :] = tin[...]
-
-    G.z_step(1, True)
-
-    NB = 2 * X * 2
-
-    @pl.loop(0, NB)
-    def _(b):
-        off = pl.multiple_of(b * T, T)
-        lanes = lax.broadcasted_iota(jnp.int32, (CAP, T), 1) + b * T
-        oh[:, pl.ds(off, T)] = jnp.where(rows_col[...] == lanes, 1.0, 0.0).astype(BF)
-        subs = lax.broadcasted_iota(jnp.int32, (T, CAP), 0) + b * T
-        oht[pl.ds(off, T), :] = jnp.where(rows_row[...] == subs, 1.0, 0.0).astype(BF)
-
-    G.z_step(2, True)
-    W.z_step(1, False)
-    x_arrivals(zh)
-    tok_leg2()
-    G.z_step(3, True)
-    W.z_step(2, False)
-    G.relay_step(0)
-    W.y_step(0)
-    x_far(zh)
-    G.z_step(4, True)
-    W.z_step(3, False)
-    G.relay_step(1)
-    W.y_step(1)
-    tok_opp()
-    G.z_step(5, True)
-    W.z_step(4, False)
-    G.relay_step(2)
-    W.y_step(2)
-    G.z_step(6, True)
-    W.z_step(5, False)
-    G.relay_step(3)
-    W.y_step(3)
-    x_arrivals(oz)
-    G.z_step(7, True)
-    W.z_step(6, False)
-    G.relay_step(4)
-    W.y_step(4)
-    W.z_step(7, False)
-    G.relay_step(5)
-    W.y_step(5)
-    x_far(oz)
-
-    @pl.loop(6, 8)
+            f(s - lo)
+
+    DL, A0, B0, RL = 3, 1, 2, 2
+
+    def when_at(s, lag, f):
+        v = s - (A0 + lag)
+
+        @pl.when((v >= 0) & (v % B0 == 0) & (v // B0 < NP))
+        def _():
+            f(v // B0)
+
+    def dn_start(_):
+        for d in range(2):
+            @pl.when(has_z[d])
+            def _():
+                W.z_send(dn_in, k, d)
+        W.y_send(dn_in, k)
+
+    def step(s):
+        when_in(s, 1, ZL, lambda i: G.z_step(i + 1, True))
+        when_at(s, 0, leg1)
+        when_at(s, 1, leg2)
+        when_in(s, DL, DL + 1, dn_start)
+        when_in(s, DL + 1, DL + ZL, lambda i: W.z_step(i + 1, True))
+        when_in(s, 1, 2, lambda i: own_arrivals())
+        when_at(s, 2, opp_arrived)
+        when_in(s, RL, RL + ZL, G.relay_step)
+        when_in(s, 2, 3, lambda i: own_far())
+        when_at(s, 3, opp_x)
+        when_at(s, 4, opp_far)
+        when_in(s, DL + RL, DL + RL + ZL, W.relay_step)
+
+    TN = min(256, D)
+    NT = D // TN
+    HG = 2 * X * T
+
+    def pick(n, q, first):
+        cols = pl.ds(pl.multiple_of(n * TN, TN), TN)
+        ks = pl.ds(pl.multiple_of(q * HG, HG), HG)
+        got = jnp.dot(oh[:, ks], tok[ks, cols], preferred_element_type=F32)
+        if not first:
+            got = got + picked[:, cols].astype(F32)
+        picked[:, cols] = got.astype(BF)
+
+    @pl.loop(1, 2)
     def _(s):
-        G.relay_step(s)
-        W.y_step(s)
+        step(s)
+
+    hots()
+
+    @pl.loop(2, 6)
+    def _(s):
+        step(s)
 
     for r in range(X):
-        for q in range(2):
-            wait_on(blk(1 - c, (x + r) % X, q), psem.at[1, r * 2 + q])
-
-    TN = min(256, D)
-
-    @pl.loop(0, D // TN)
+        wait_on(blk(1 - c, (x + r) % X, zh), pown.at[1, r])
+
+    @pl.loop(0, NT)
     def _(n):
-        cols = pl.ds(pl.multiple_of(n * TN, TN), TN)
-        picked[:, cols] = jnp.dot(oh[...], tok[:, cols], preferred_element_type=F32).astype(BF)
-
-    @pl.loop(0, 4)
+        pick(n, zh, True)
+
+    TAIL = A0 + 3 * B0 + 5
+
+    @pl.loop(6, TAIL)
     def _(s):
-        W.relay_step(s)
+        step(s)
+
+    @pl.loop(0, NP)
+    def _(p):
+        for r in range(X):
+            for h in range(2):
+                wait_on(piece(1 - c, (x + r) % X, oz, h, p), psem.at[1, r * 2 + h, p])
+
+    @pl.loop(0, NT)
+    def _(n):
+        pick(n, oz, False)
+
+    @pl.loop(TAIL, DL + RL + ZL)
+    def _(s):
+        step(s)
 
     G.arrived()
     TH = min(256, H)
@@ -293,10 +360,6 @@
         ga = jnp.dot(picked[...], gu[:, pl.ds(pl.multiple_of(n * TH, TH), TH)], preferred_element_type=F32)
         ub = jnp.dot(picked[...], gu[:, pl.ds(pl.multiple_of(H + n * TH, TH), TH)], preferred_element_type=F32)
         hidden[:, pl.ds(pl.multiple_of(n * TH, TH), TH)] = (ga / (1.0 + jnp.exp(-ga)) * ub).astype(BF)
-
-    @pl.loop(4, 8)
-    def _(s):
-        W.relay_step(s)
 
     W.arrived()
 
@@ -375,13 +438,22 @@
     G.drain()
     W.drain()
     for d in range(2):
-        wait_sent_on(rz.at[d], tsem.at[0, d])
-        wait_sent_on(rz.at[d], tsem.at[2, d])
-    for q in range(2):
-        for i in (0, 1, 4):
-            wait_sent_on(tin, xsem.at[i, q])
-        for r in range(X):
-            wait_sent_on(tin, psem.at[0, r * 2 + q])
+        wait_sent_on(tin, xown.at[0, d])
+        wait_sent_on(half(tin, d), xown.at[2, d])
+    for r in range(X):
+        wait_sent_on(tin, pown.at[0, r])
+
+    @pl.loop(0, NP)
+    def _(p):
+        ref = tin.at[pl.ds(0, TP)]
+        for h in range(2):
+            wait_sent_on(ref, lsem.at[0, h, p])
+            wait_sent_on(ref, lsem.at[2, h, p])
+            wait_sent_on(ref, xsem.at[0, h, p])
+            wait_sent_on(ref, xsem.at[1, h, p])
+            wait_sent_on(ref, rsem.at[0, h, p])
+            for r in range(X):
+                wait_sent_on(ref, psem.at[0, r * 2 + h, p])
 
     @pl.loop(0, NC)
     def _(n):
@@ -399,11 +471,7 @@
     CAP = choice_rows.shape[2]
     group = 4 * X * T
     CW = D // NC
-    rows = choice_rows[0, 0]
-    dev, r = rows // T, rows % T
-    zh, x, c = dev // (2 * X), (dev // 2) % X, dev % 2
-    rows = (c * (2 * X) + x * 2 + zh) * T + r
-    gu_in = jnp.concatenate([w_gate[0], w_up[0]], axis=1)
+    K = w_gate.shape[1]
     dn_in = w_down[0]
     dps = Y * ZL
     vmem = pl.BlockSpec(memory_space=pltpu.VMEM)
@@ -413,8 +481,9 @@
         in_specs=[vmem] * 6,
         out_specs=vmem,
         scratch_shapes=[
+            pltpu.VMEM((CAP, 1), F32),
             pltpu.VMEM((group, D), BF),
-            pltpu.VMEM((dps * gu_in.shape[0], 2 * H), BF),
+            pltpu.VMEM((dps * K, 2 * H), BF),
             pltpu.VMEM((dps * dn_in.shape[0], D), BF),
             pltpu.VMEM((CAP, group), BF),
             pltpu.VMEM((group, CAP), BF),
@@ -431,15 +500,18 @@
             pltpu.VMEM((NC, T, CW), BF),
             pltpu.SemaphoreType.DMA((11, ZL)),
             pltpu.SemaphoreType.DMA((11, ZL)),
+            pltpu.SemaphoreType.DMA((4, 2, NP)),
+            pltpu.SemaphoreType.DMA((4, 2, NP)),
+            pltpu.SemaphoreType.DMA((2, 2, NP)),
+            pltpu.SemaphoreType.DMA((2, 2 * X, NP)),
             pltpu.SemaphoreType.DMA((4, 2)),
-            pltpu.SemaphoreType.DMA((6, 2)),
-            pltpu.SemaphoreType.DMA((2, 8)),
+            pltpu.SemaphoreType.DMA((2, X)),
             pltpu.SemaphoreType.DMA((NC, 18)),
         ],
         compiler_params=pltpu.CompilerParams(
             collective_id=0, has_side_effects=True, vmem_limit_bytes=62 * 1024 * 1024
         ),
-    )(tokens, gu_in, dn_in, rows.reshape(CAP, 1), rows.reshape(1, CAP), gate_weights.reshape(CAP, 1))
+    )(tokens, w_gate[0], w_up[0], dn_in, choice_rows[0], gate_weights[0])
 
 
 def solution(mesh):

time: 255 us -> 231 us (0.906)
  the two profiles are of different devices: /device:TPU:24 before, /device:TPU:118 now
where the time goes in v2:
time: 231 us
  Pallas kernels  229 us (99%)
    pallas_call x1, Pallas kernels, per_device(): pl.pallas_call(functools.partial(layer_kernel, ZL), out_shape=jax.ShapeDt...  229 us

profile of v2, /device:TPU:118, one launch (start us, length us, event | category | flops | bytes accessed | tf_op | source)
XLA Modules:
  0.0 230.7 jit_solution(4616041558765699418)
XLA Ops:
  0.0 228.8 %shard_map.64 = bf16[128,2048]{1,0:T(8,128)(2,1)} custom-call(bf16[128,2048]{1,0:T(8,128)(2,1)} %tin.1, bf16[64,1024]{1,0:T(8,128)(2,1)} %bitcast.5, bf16[64,1024]{1,0:T(8,128)(2,1)} %bitcast.6, bf16[32,2048]{1,0:T(8,128)(2,1)} %bitcast.7, s32[1,512]{1,0:T(1,128)} %bitcast.8, f32[1,512]{1,0:T(1,128)} %bitcast.9), custom_call_target="tpu_custom_call" | custom-call | tf_op jit(solution)/shard_map/pallas_call | solution.py:478
  228.8 1.9 copy.8

commit v3 on v2

--- a/solution.py
+++ b/solution.py
@@ -10,7 +10,8 @@
 MESH = pl.DeviceIdType.MESH
 Y = 4
 X = 4
-NC = 4
+NC = 8
+LAGS = (0, 1, 2, 3, 5, 7)
 NP = 4
 BF = jnp.bfloat16
 F32 = jnp.float32
@@ -33,7 +34,7 @@
     out,
     gw_col, tok, gu, dn, oh, oht, picked, hidden, contrib, dense,
     rz, prcv, xrl, xf, zsend, zrel, zfin,
-    gsem, dsem, lsem, xsem, rsem, psem, xown, pown, csem,
+    gsem, dsem0, dsem1, lsem, xsem, rsem, psem, xown, pown, csem,
 ):
     T, D = tin.shape
     H = gu.shape[1] // 2
@@ -157,7 +158,8 @@
                         self.wait_sent(ref, 1 + d, j)
 
     G = Part(gu_own, gu, gsem)
-    W = Part(dn_in, dn, dsem)
+    D2 = D // 2
+    WS = tuple(Part(dn_in.at[:, pl.ds(i * D2, D2)], dn.at[i], m) for i, m in enumerate((dsem0, dsem1)))
 
     def blk(c_, x_, q_):
         b = q_ * (2 * X) + c_ * X + x_
@@ -243,7 +245,8 @@
     G.y_send(gu_own, k)
     own_start()
 
-    dn[pl.ds(pl.multiple_of(dp * dn_in.shape[0], dn_in.shape[0]), dn_in.shape[0]), :] = dn_in[...]
+    for i in range(2):
+        dn[i, pl.ds(pl.multiple_of(dp * dn_in.shape[0], dn_in.shape[0]), dn_in.shape[0]), :] = dn_in[:, i * D2 : (i + 1) * D2]
     tok[pl.ds(pl.multiple_of((zh * 2 * X + c * X + x) * T, T), T), :] = tin[...]
 
     NB = 2 * X * 2
@@ -273,6 +276,7 @@
         def _():
             f(s - lo)
 
+    D1 = 3
     DL, A0, B0, RL = 3, 1, 2, 2
 
     def when_at(s, lag, f):
@@ -282,26 +286,30 @@
         def _():
             f(v // B0)
 
-    def dn_start(_):
-        for d in range(2):
-            @pl.when(has_z[d])
-            def _():
-                W.z_send(dn_in, k, d)
-        W.y_send(dn_in, k)
+    def dn_step(W, s, lag):
+        @pl.when(s == lag)
+        def _():
+            for d in range(2):
+                @pl.when(has_z[d])
+                def _():
+                    W.z_send(W.own, k, d)
+            W.y_send(W.own, k)
+
+        when_in(s, lag + 1, lag + ZL, lambda i: W.z_step(i + 1, True))
+        when_in(s, lag + RL, lag + RL + ZL, W.relay_step)
 
     def step(s):
         when_in(s, 1, ZL, lambda i: G.z_step(i + 1, True))
         when_at(s, 0, leg1)
         when_at(s, 1, leg2)
-        when_in(s, DL, DL + 1, dn_start)
-        when_in(s, DL + 1, DL + ZL, lambda i: W.z_step(i + 1, True))
         when_in(s, 1, 2, lambda i: own_arrivals())
         when_at(s, 2, opp_arrived)
         when_in(s, RL, RL + ZL, G.relay_step)
         when_in(s, 2, 3, lambda i: own_far())
         when_at(s, 3, opp_x)
         when_at(s, 4, opp_far)
-        when_in(s, DL + RL, DL + RL + ZL, W.relay_step)
+        dn_step(WS[0], s, DL)
+        dn_step(WS[1], s, DL + D1)
 
     TN = min(256, D)
     NT = D // TN
@@ -333,6 +341,7 @@
         pick(n, zh, True)
 
     TAIL = A0 + 3 * B0 + 5
+    END = DL + RL + ZL
 
     @pl.loop(6, TAIL)
     def _(s):
@@ -348,7 +357,7 @@
     def _(n):
         pick(n, oz, False)
 
-    @pl.loop(TAIL, DL + RL + ZL)
+    @pl.loop(TAIL, max(END, TAIL))
     def _(s):
         step(s)
 
@@ -361,14 +370,14 @@
         ub = jnp.dot(picked[...], gu[:, pl.ds(pl.multiple_of(H + n * TH, TH), TH)], preferred_element_type=F32)
         hidden[:, pl.ds(pl.multiple_of(n * TH, TH), TH)] = (ga / (1.0 + jnp.exp(-ga)) * ub).astype(BF)
 
-    W.arrived()
+    WS[0].arrived()
 
     HB = 2 * X * T
     TM = min(256, HB)
 
     def s1(n):
-        cols = pl.ds(pl.multiple_of(n * CW, CW), CW)
-        o = jnp.dot(hidden[...], dn[:, cols], preferred_element_type=F32)
+        cols2 = pl.ds(pl.multiple_of((n % (NC // 2)) * CW, CW), CW)
+        o = jnp.dot(hidden[...], dn[n // (NC // 2), :, cols2], preferred_element_type=F32)
         contrib[...] = (gw_col[...] * o).astype(BF)
 
         def spread(base):
@@ -428,15 +437,26 @@
 
     stages = (s1, s2, s3, s4, s5, s6)
 
-    @pl.loop(0, NC + len(stages) - 1)
+    BEG = max(END, TAIL)
+
+    @pl.loop(0, NC + LAGS[-1])
     def _(t):
+        @pl.when(t < D1)
+        def _():
+            dn_step(WS[1], t + BEG, DL + D1)
+
+        @pl.when(t == NC // 2)
+        def _():
+            WS[1].arrived()
+
         for i in reversed(range(len(stages))):
-            @pl.when((t >= i) & (t < NC + i))
+            @pl.when((t >= LAGS[i]) & (t < NC + LAGS[i]))
             def _():
-                stages[i](t - i)
+                stages[i](t - LAGS[i])
 
     G.drain()
-    W.drain()
+    WS[0].drain()
+    WS[1].drain()
     for d in range(2):
         wait_sent_on(tin, xown.at[0, d])
         wait_sent_on(half(tin, d), xown.at[2, d])
@@ -484,7 +504,7 @@
             pltpu.VMEM((CAP, 1), F32),
             pltpu.VMEM((group, D), BF),
             pltpu.VMEM((dps * K, 2 * H), BF),
-            pltpu.VMEM((dps * dn_in.shape[0], D), BF),
+            pltpu.VMEM((2, dps * dn_in.shape[0], D // 2), BF),
             pltpu.VMEM((CAP, group), BF),
             pltpu.VMEM((group, CAP), BF),
             pltpu.VMEM((CAP, D), BF),
@@ -500,6 +520,7 @@
             pltpu.VMEM((NC, T, CW), BF),
             pltpu.SemaphoreType.DMA((11, ZL)),
             pltpu.SemaphoreType.DMA((11, ZL)),
+            pltpu.SemaphoreType.DMA((11, ZL)),
             pltpu.SemaphoreType.DMA((4, 2, NP)),
             pltpu.SemaphoreType.DMA((4, 2, NP)),
             pltpu.SemaphoreType.DMA((2, 2, NP)),

time: 231 us -> 211 us (0.913)
  the two profiles are of different devices: /device:TPU:118 before, /device:TPU:24 now
where the time goes in v3:
time: 211 us; the launch traced here: 209 us
  Pallas kernels  208 us (99%)
    pallas_call x1, Pallas kernels, per_device(): pl.pallas_call(functools.partial(layer_kernel, ZL), out_shape=jax.ShapeDt...  208 us

profile of v3, /device:TPU:24, one launch (start us, length us, event | category | flops | bytes accessed | tf_op | source)
XLA Modules:
  0.0 209.5 jit_solution(5708970639198815881)
XLA Ops:
  0.0 207.6 %shard_map.64 = bf16[128,2048]{1,0:T(8,128)(2,1)} custom-call(bf16[128,2048]{1,0:T(8,128)(2,1)} %tin.1, bf16[64,1024]{1,0:T(8,128)(2,1)} %bitcast.5, bf16[64,1024]{1,0:T(8,128)(2,1)} %bitcast.6, bf16[32,2048]{1,0:T(8,128)(2,1)} %bitcast.7, s32[1,512]{1,0:T(1,128)} %bitcast.8, f32[1,512]{1,0:T(1,128)} %bitcast.9), custom_call_target="tpu_custom_call" | custom-call | tf_op jit(solution)/shard_map/pallas_call | solution.py:498
  207.6 1.9 copy.8

commit v4 on v3

--- a/solution.py
+++ b/solution.py
@@ -397,14 +397,16 @@
     def s2(n):
         wait_on(prcv.at[n], csem.at[n, 1])
 
-        @pl.loop(0, 2 * X)
-        def _(b):
+        def add(i):
+            b = (x2 * 2 + i) % (2 * X)
             r = pl.ds(pl.multiple_of(b * T, T), T)
             mine = dense[n, pl.ds(pl.multiple_of(c * HB + b * T, T), T), :]
             prcv[n, r, :] = (prcv[n, r, :].astype(F32) + mine.astype(F32)).astype(BF)
 
+        pl.loop(0, 2)(add)
         for d in range(2):
             remote(pblk(n, x2, d), xrl.at[d, n], csem.at[n, 2 + d], csem.at[n, 4 + d], dev_x[d]).start()
+        pl.loop(2, 2 * X)(add)
 
     def s3(n):
         for d, x_ in ((0, xp), (1, xm)):

time: 211 us -> 213 us (level)
  no operation moved by 1% of the time
where the time goes in v4:
time: 213 us; the launch traced here: 210 us
  Pallas kernels  208 us (98%)
    pallas_call x1, Pallas kernels, per_device(): pl.pallas_call(functools.partial(layer_kernel, ZL), out_shape=jax.ShapeDt...  208 us

profile of v4, /device:TPU:24, one launch (start us, length us, event | category | flops | bytes accessed | tf_op | source)
XLA Modules:
  0.0 209.9 jit_solution(620985298660120306)
XLA Ops:
  0.0 208.0 %shard_map.64 = bf16[128,2048]{1,0:T(8,128)(2,1)} custom-call(bf16[128,2048]{1,0:T(8,128)(2,1)} %tin.1, bf16[64,1024]{1,0:T(8,128)(2,1)} %bitcast.5, bf16[64,1024]{1,0:T(8,128)(2,1)} %bitcast.6, bf16[32,2048]{1,0:T(8,128)(2,1)} %bitcast.7, s32[1,512]{1,0:T(1,128)} %bitcast.8, f32[1,512]{1,0:T(1,128)} %bitcast.9), custom_call_target="tpu_custom_call" | custom-call | tf_op jit(solution)/shard_map/pallas_call | solution.py:500
  208.0 1.9 copy.8
